TPU v7x, 32 devices: a whole 2x2x4 slice. The times are simulated.
32 devices in a mesh: batch: 4 (over x, core), centers: 8 (over z, y).
Axes of the slice: x: 2, y: 2, z: 4, core: 2. Of those that a mesh axis runs over, the one named last changes fastest.
Arguments:
- pool_features: float32 [32768, 128], P(('batch', 'centers')), may hold values from -14 to 14
- pool_targets: float32 [32768, 64], P(('batch', 'centers')), may hold values from -6 to 6
- batch_index: int32 [2048], P(('batch', 'centers')), may hold values from 0 to 1023
- centers: float32 [4096, 128], P('centers'), may hold values from -14 to 14
- weights: float32 [4096, 64], P('centers'), as said below
- eig_vectors: float32 [4096, 1024], P(('batch', 'centers')), may hold values from -0.09375 to 0.09375
- eig_scale: float32 [1024], replicated, may hold values from 0.5 to 4
- nys_owner: int32 [4096, 1], P(('batch', 'centers')), may hold values from 0 to 7; in each aligned block of 128 rows (0 to 127, 128 to 255, ...) at most 32 rows name the same one
- nys_offset: int32 [4096], P(('batch', 'centers')), may hold values from 0 to 511
Outputs:
- residual_out: float32 [2048, 64], P(('batch', 'centers'))
- update: float32 [4096, 64], P('centers')
Inputs may be any that keep to these rules, and one draw needn't show every extreme that they name: `nys_owner`: among the 128 rows of one device no owner is named more than 32 times; on some devices one owner is named exactly 32 times. `weights`: every column sums to zero.
All inputs are finite; a program needn't handle non-finite values.
Results may differ from a plain program's by a relative error of at most 0.0003.
Values sent between devices are 32-bit elements; how exact they have to be, the bound alone decides.
A program may use at most 64 MiB of HBM per device.

v0:
```python
import math
import jax
import jax.numpy as jnp
from jax import lax
from jax.sharding import PartitionSpec as P

DEPTH = 3
epsilon = 1e-06
highest = lax.Precision.HIGHEST


def kernel_rows(row_block, center_block, center_norm):
    inner_prod = (
        lax.dot_general(
            row_block,
            center_block,
            (((1,), (1,)), ((), ())),
            precision=highest,
            preferred_element_type=jnp.float32,
        )
        / row_block.shape[1]
    )
    row_norm = jnp.mean(row_block * row_block, axis=1) + epsilon
    norm_scale = jnp.sqrt(row_norm[:, None] * center_norm[None, :])
    sigma_now = inner_prod
    tangent = inner_prod
    for depth_step in range(DEPTH):
        cosine = sigma_now / norm_scale
        arc_angle = jnp.arccos(cosine)
        remain = (math.pi - arc_angle) / math.pi
        sigma_now = (
            norm_scale
            * (jnp.sqrt(1.0 - cosine * cosine) + (math.pi - arc_angle) * cosine)
            / math.pi
        )
        tangent = sigma_now + tangent * remain
    return tangent


def per_device(
    pool_features,
    pool_targets,
    batch_index,
    centers,
    weights,
    eig_vectors,
    eig_scale,
    nys_owner,
    nys_offset,
):
    local_rows = pool_features[batch_index]
    local_targets = pool_targets[batch_index]
    row_count = local_rows.shape[0]
    group_size = lax.axis_size("centers")
    rows_total = row_count * group_size * lax.axis_size("batch")
    center_count = centers.shape[0]
    outputs = weights.shape[1]
    center_norm = jnp.mean(centers * centers, axis=1) + epsilon
    kernel = kernel_rows(
        lax.all_gather(local_rows, "centers", axis=0, tiled=True), centers, center_norm
    )
    partial_pred = jnp.dot(kernel, weights, precision=highest, preferred_element_type=jnp.float32)
    all_targets = lax.all_gather(local_targets, "centers", axis=0, tiled=True)
    prediction = lax.psum(partial_pred, "centers")
    residual = prediction - all_targets
    own_residual = lax.dynamic_slice_in_dim(
        residual, lax.axis_index("centers") * row_count, row_count, 0
    )
    grads_part = lax.dot_general(
        kernel,
        residual,
        (((0,), (0,)), ((), ())),
        precision=highest,
        preferred_element_type=jnp.float32,
    ) / math.sqrt(rows_total)
    grads = lax.psum(grads_part, "batch")
    owner = nys_owner[:, 0]
    slots = max(2, 2 * owner.shape[0] // group_size)
    owner_hot = (owner[:, None] == jnp.arange(group_size, dtype=jnp.int32)[None, :]).astype(
        jnp.int32
    )
    slot_rank = jnp.sum((jnp.cumsum(owner_hot, axis=0) - owner_hot) * owner_hot, axis=1)
    requests = jnp.zeros((group_size, slots), jnp.int32).at[owner, slot_rank].set(nys_offset)
    received = lax.all_to_all(requests, "centers", split_axis=0, concat_axis=0, tiled=True)
    found = grads[received]
    returned = lax.all_to_all(found, "centers", split_axis=0, concat_axis=0, tiled=True)
    picked_grads = returned[owner, slot_rank]
    coeff_part = lax.dot_general(
        eig_vectors,
        picked_grads,
        (((0,), (0,)), ((), ())),
        precision=highest,
        preferred_element_type=jnp.float32,
    )
    coeff = lax.psum(coeff_part, ("batch", "centers"))
    corr_rows = jnp.dot(
        eig_vectors,
        eig_scale[:, None] * coeff,
        precision=highest,
        preferred_element_type=jnp.float32,
    )
    outgoing = (
        jnp.zeros((group_size, slots, outputs), jnp.float32).at[owner, slot_rank].set(corr_rows)
    )
    incoming = lax.all_to_all(outgoing, "centers", split_axis=0, concat_axis=0, tiled=True)
    corr_part = jnp.zeros((center_count, outputs), jnp.float32).at[received].add(incoming)
    correction = lax.psum(corr_part, "batch")
    return (own_residual, correction - grads)


def solution(mesh):
    placed = (
        P(("batch", "centers"), None),
        P(("batch", "centers"), None),
        P(("batch", "centers")),
        P("centers", None),
        P("centers", None),
        P(("batch", "centers"), None),
        P(),
        P(("batch", "centers"), None),
        P(("batch", "centers")),
    )
    return jax.shard_map(
        per_device,
        mesh=mesh,
        in_specs=placed,
        out_specs=(P(("batch", "centers"), None), P("centers", None)),
        check_vma=False,
    )
```

profile of v0, /device:TPU:0, one launch (start us, length us, event | category | flops | bytes accessed | tf_op | source)
XLA Modules:
  0.0 387.0 jit_solution(5106888059048131326)
XLA Ops:
  7.2 0.0 copy-start
  7.2 0.0 copy-start.6
  7.2 0.7 copy-done.6
  7.9 0.1 fusion.4
  8.0 0.2 reduce_window_sum.11
  8.2 0.2 select_reduce_fusion
  8.3 0.0 copy-start.8
  8.4 0.6 broadcast.104
  9.0 0.1 copy-done.8
  9.0 19.9 %scatter_fusion = s32[8,32]{1,0:T(8,128)} fusion(s32[8,32]{1,0:T(8,128)} %broadcast.104, s32[128]{0:T(128)S(1)} %get-tuple-element.8, s32[128]{0:T(128)S(1)} %copy-done.8), kind=kCustom, calls=%fused_computation.4 | custom fusion | bytes 2560 | tf_op jit(solution)/shard_map/scatter | solution.py:83
  28.9 7.4 %all-to-all-start = ((s32[8,1,32]{2,1,0:T(1,128)}), s32[8,1,32]{2,1,0:T(1,128)S(1)}, u32[]{:S(2)}, u32[]{:S(2)}) async-start(s32[8,1,32]{2,1,0:T(1,128)} %bitcast.4), calls=%async_computation | async-start | bytes 8192 | tf_op jit(solution)/shard_map/all_to_all | solution.py:84
  36.3 0.0 all-reduce.5.cloned.1.call-start
  36.4 0.0 copy-done.9
  36.4 0.1 multiply_reduce_fusion
  36.6 0.6 gather_fusion
  37.2 31.2 %all-gather = f32[512,128]{1,0:T(8,128)S(1)} all-gather(f32[64,128]{1,0:T(8,128)S(1)} %gather_fusion), channel_id=2, replica_groups=mesh['batch'=4,'centers'=8] {'centers'}, dimensions={0}, use_global_device_ids=true | all-gather | bytes 294912 | tf_op jit(solution)/shard_map/all_gather | solution.py:60
  68.4 0.1 multiply_reduce_fusion.1
  68.6 0.0 copy-start.4
  68.6 8.9 %multiply_add_fusion = f32[512,512]{1,0:T(8,128)S(1)} fusion(f32[512,128]{1,0:T(8,128)S(1)} %all-gather, f32[512,128]{1,0:T(8,128)S(1)} %copy-done.3, f32[512]{0:T(512)S(1)} %multiply_add_fusion.1, f32[512]{0:T(512)S(1)} %multiply_add_fusion.2), kind=kOutput, calls=%fused_computation.11 | convolution fusion | flops 414187520 | bytes 1576960 | tf_op jit(solution)/shard_map/dot_general | solution.py:14
  77.5 0.0 copy-start.2
  77.5 1.8 fusion.8
  79.3 0.0 all-reduce.5.cloned.1.call-update
  79.4 0.0 all-reduce.7.cloned.1.call-start
  79.4 0.2 copy.23
  79.6 0.6 gather_fusion.1
  80.2 30.8 %all-gather.1 = f32[512,64]{1,0:T(8,128)S(1)} all-gather(f32[64,64]{1,0:T(8,128)S(1)} %gather_fusion.1), channel_id=3, replica_groups=mesh['batch'=4,'centers'=8] {'centers'}, dimensions={0}, use_global_device_ids=true | all-gather | bytes 147456 | tf_op jit(solution)/shard_map/all_gather | solution.py:63
  111.1 0.1 copy.24
  111.2 0.0 all-to-all-done
  111.2 0.1 reshape.100
  111.3 39.5 %all-reduce.5.cloned.1.call-done = f32[512,64]{0,1:T(8,128)} async-done(((f32[512,64]{0,1:T(8,128)}), f32[512,64]{0,1:T(8,128)}) %all-reduce.5.cloned.1.call-update) | async-done | bytes 131088 | tf_op jit(solution)/shard_map/psum | solution.py:64
  150.8 0.9 sub.36
  151.7 1.5 convolution_multiply_fusion.1
  153.2 0.0 all-reduce.7.cloned.1.call-update
  153.2 0.0 all-reduce.9.cloned.1.call-start
  153.3 31.3 %all-reduce.7.cloned.1.call-done = f32[512,64]{0,1:T(8,128)} async-done(((f32[512,64]{0,1:T(8,128)}), f32[512,64]{0,1:T(8,128)}) %all-reduce.7.cloned.1.call-update) | async-done | bytes 131088 | tf_op jit(solution)/shard_map/psum | solution.py:76
  184.6 1.0 copy.26
  185.6 0.7 gather_fusion.2
  186.3 0.1 reshape.114
  186.5 12.2 %all_to_all.22 = f32[8,1,2048]{2,1,0:T(1,128)S(1)} all-to-all(f32[8,1,2048]{2,1,0:T(1,128)S(1)} %reshape.114), channel_id=1, replica_groups=mesh['batch'=4,'centers'=8] {'centers'}, dimensions={0} | all-to-all | bytes 131072 | tf_op jit(solution)/shard_map/all_to_all | solution.py:86
  198.7 0.5 broadcast.212
  199.2 0.8 reduce
  200.0 0.1 reshape.115
  200.1 1.2 gather_fusion.3
  201.3 0.0 copy-done
  201.3 1.1 convolution_bitcast_fusion
  202.5 0.0 all-reduce.9.cloned.1.call-update
  202.5 123.4 %all-reduce.9.cloned.1.call-done = f32[1024,64]{0,1:T(8,128)} async-done(((f32[1024,64]{0,1:T(8,128)}), f32[1024,64]{0,1:T(8,128)}) %all-reduce.9.cloned.1.call-update) | async-done | bytes 262160 | tf_op jit(solution)/shard_map/psum | solution.py:95
  325.9 1.6 convolution_bitcast_fusion.1
  327.5 0.1 copy.27
  327.7 6.9 %scatter_fusion.1 = f32[8,32,64]{2,1,0:T(8,128)S(1)} fusion(f32[8,32,64]{2,1,0:T(8,128)S(1)} %broadcast_in_dim.8, s32[128]{0:T(128)S(1)} %get-tuple-element.8, f32[128,64]{1,0:T(8,128)S(1)} %copy.27), kind=kCustom, calls=%fused_computation.5 | custom fusion | bytes 99328 | tf_op jit(solution)/shard_map/scatter | solution.py:103
  334.6 0.8 reshape.116
  335.3 4.5 %all-to-all-start.2 = ((f32[8,1,2048]{2,1,0:T(1,128)}), f32[8,1,2048]{2,1,0:T(1,128)S(1)}, u32[]{:S(2)}, u32[]{:S(2)}) async-start(f32[8,1,2048]{2,1,0:T(1,128)} %reshape.116), calls=%async_computation.2 | async-start | bytes 131072 | tf_op jit(solution)/shard_map/all_to_all | solution.py:105
  339.8 0.0 all-reduce.11.cloned.1.call-start
  339.9 6.9 %all-to-all-done.2 = f32[8,1,2048]{2,1,0:T(1,128)S(1)} async-done(((f32[8,1,2048]{2,1,0:T(1,128)}), f32[8,1,2048]{2,1,0:T(1,128)S(1)}, u32[]{:S(2)}, u32[]{:S(2)}) %all-to-all-start.2) | async-done | bytes 65568 | tf_op jit(solution)/shard_map/all_to_all | solution.py:105
  346.7 0.8 reduce.1
  347.6 0.1 reshape.117
  347.6 1.7 scatter_custom_fusion.2
  349.4 0.8 copy.28
  350.2 0.0 all-reduce.11.cloned.1.call-update
  350.2 0.1 constant_dynamic-slice_fusion
  350.3 0.7 copy.29
  351.0 27.9 %all-reduce.11.cloned.1.call-done = f32[512,64]{0,1:T(8,128)} async-done(((f32[512,64]{0,1:T(8,128)}), f32[512,64]{0,1:T(8,128)}) %all-reduce.11.cloned.1.call-update) | async-done | bytes 131088 | tf_op jit(solution)/shard_map/psum | solution.py:107
  378.9 0.0 copy-done.1
  378.9 1.6 sub.38
  (18 shorter events, 0.1 us)
Async XLA Ops:
  7.2 194.2 %copy-start = (f32[128,1024]{1,0:T(8,128)S(1)}, f32[128,1024]{1,0:T(8,128)}, u32[]{:S(2)}) copy-start(f32[128,1024]{1,0:T(8,128)} %param.14) | copy-start | bytes 1572868
  7.2 0.7 copy-start.6
  8.3 0.7 copy-start.8
  9.0 27.4 %copy-start.3 = (f32[512,128]{1,0:T(8,128)S(1)}, f32[512,128]{1,0:T(8,128)}, u32[]{:S(2)}) copy-start(f32[512,128]{1,0:T(8,128)} %param.12) | copy-start | bytes 786436
  9.0 27.6 %copy-start.5 = (f32[1024,128]{1,0:T(8,128)S(1)}, f32[1024,128]{1,0:T(8,128)}, u32[]{:S(2)}) copy-start(f32[1024,128]{1,0:T(8,128)} %param.9) | copy-start | bytes 1572868
  28.9 7.5 %copy-start.9 = (s32[64]{0:T(128)S(1)}, s32[64]{0:T(128)}, u32[]{:S(2)}) copy-start(s32[64]{0:T(128)} %param.11) | copy-start | bytes 772
  28.9 82.3 %all-to-all-start = ((s32[8,1,32]{2,1,0:T(1,128)}), s32[8,1,32]{2,1,0:T(1,128)S(1)}, u32[]{:S(2)}, u32[]{:S(2)}) async-start(s32[8,1,32]{2,1,0:T(1,128)} %bitcast.4), calls=%async_computation | async-start | bytes 8192 | tf_op jit(solution)/shard_map/all_to_all | solution.py:84
  36.3 114.5 %all-reduce.5.cloned.1.call-start = ((), (), s32[]{:S(2)}) async-start(), calls=%async_computation.3 | async-start | bytes 262144 | tf_op jit(solution)/shard_map/psum | solution.py:64
  68.6 8.9 %copy-start.4 = (f32[512,64]{0,1:T(8,128)S(1)}, f32[512,64]{0,1:T(8,128)}, u32[]{:S(2)}) copy-start(f32[512,64]{0,1:T(8,128)} %param.13) | copy-start | bytes 393220
  77.5 1.9 copy-start.2
  79.4 105.2 %all-reduce.7.cloned.1.call-start = ((), (), s32[]{:S(2)}) async-start(), calls=%async_computation.4 | async-start | bytes 262144 | tf_op jit(solution)/shard_map/psum | solution.py:76
  153.2 172.7 %all-reduce.9.cloned.1.call-start = ((), (), s32[]{:S(2)}) async-start(), calls=%async_computation.5 | async-start | bytes 524288 | tf_op jit(solution)/shard_map/psum | solution.py:95
  202.5 123.4 %copy-start.7 = (f32[1024]{0:T(1024)S(1)}, f32[1024]{0:T(1024)}, u32[]{:S(2)}) copy-start(f32[1024]{0:T(1024)} %param.15) | copy-start | bytes 12292
  335.3 11.4 %all-to-all-start.2 = ((f32[8,1,2048]{2,1,0:T(1,128)}), f32[8,1,2048]{2,1,0:T(1,128)S(1)}, u32[]{:S(2)}, u32[]{:S(2)}) async-start(f32[8,1,2048]{2,1,0:T(1,128)} %reshape.116), calls=%async_computation.2 | async-start | bytes 131072 | tf_op jit(solution)/shard_map/all_to_all | solution.py:105
  339.8 39.0 %all-reduce.11.cloned.1.call-start = ((), (), s32[]{:S(2)}) async-start(), calls=%async_computation.6 | async-start | bytes 262144 | tf_op jit(solution)/shard_map/psum | solution.py:107
  350.1 28.7 %copy-start.1 = (f32[512,64]{0,1:T(8,128)S(1)}, f32[512,64]{0,1:T(8,128)}, u32[]{:S(2)}) copy-start(f32[512,64]{0,1:T(8,128)} %all-reduce.7.cloned.1.call-done) | copy-start | bytes 393220
Sparse Core Ops, SparseCore 0:
  79.5 71.2 all-reduce.4
  153.7 30.8 all-reduce.6
  202.6 123.2 all-reduce.8
  350.3 28.5 all-reduce.10
where the time goes:
time: 388 us; the launch traced here: 387 us
  waiting for transfers between devices  229 us (59%)
  blocking collectives  74.3 us (19%)
  local copies, waits for them, and re-layouts  36 us (9%)
  matrix products  14.9 us (4%)
  between operations  14 us (4%)
  starting transfers between devices  12.1 us (3%)
  other arithmetic  6.6 us (2%)
    psum x1, waiting for transfers between devices, per_device(): coeff = lax.psum(coeff_part, ('batch', 'centers'))  123 us
    psum x1, waiting for transfers between devices, per_device(): prediction = lax.psum(partial_pred, 'centers')  39.5 us
    psum x1, waiting for transfers between devices, per_device(): grads = lax.psum(grads_part, 'batch')  31.3 us
    all_gather x1, blocking collectives, per_device(): lax.all_gather(local_rows, 'centers', axis=0, tiled=True)  31.2 us
    all_gather x1, blocking collectives, per_device(): all_targets = lax.all_gather(local_targets, 'centers', axis=0, tiled=True)  30.8 us
    psum x1, waiting for transfers between devices, per_device(): correction = lax.psum(corr_part, 'batch')  27.9 us
    scatter x1, local copies, waits for them, and re-layouts, per_device(): jnp.zeros((group_size, slots), jnp.int32).at[owner, slot_rank]  19.9 us
    all_to_all x1, blocking collectives, per_device(): lax.all_to_all(found, 'centers', split_axis=0, concat_axis=0, tiled=True)  12.2 us
  transfers between devices with their start and end apart: 6, of which 5 were waited for; matrix products, arithmetic and copies ran while one was open for 3% of the time, Pallas kernels for 0%

commit v1 on v0

--- a/solution.py
+++ b/solution.py
@@ -92,7 +92,10 @@
         precision=highest,
         preferred_element_type=jnp.float32,
     )
-    coeff = lax.psum(coeff_part, ("batch", "centers"))
+    obtain_numbers_on_mesh = lambda body, mesh_ax, group_axis: lax.psum(
+        lax.psum(body, axis_name=mesh_ax), axis_name=group_axis
+    )
+    coeff = obtain_numbers_on_mesh(coeff_part, "centers", "batch")
     corr_rows = jnp.dot(
         eig_vectors,
         eig_scale[:, None] * coeff,

time: 388 us -> 367 us (0.946)
  waiting for transfers between devices: 229 us -> 207 us
    psum x1 -> x2, waiting for transfers between devices: 123 us -> 101 us  [the longest x1 67.7 us: per_device(): lax.psum(body, axis_name=mesh_ax)]
  transfers between devices with their start and end apart: 6 -> 7, of which waited for: 5 -> 6; matrix products, arithmetic and copies ran while one was open for 3% -> 4% of each run, Pallas kernels for 0% -> 0%
where the time goes in v1:
time: 367 us; the launch traced here: 366 us
  waiting for transfers between devices  207 us (56%)
  blocking collectives  74.3 us (20%)
  local copies, waits for them, and re-layouts  36 us (10%)
  matrix products  14.9 us (4%)
  between operations  14 us (4%)
  starting transfers between devices  13.1 us (4%)
  other arithmetic  6.6 us (2%)
    psum x1, waiting for transfers between devices, per_device(): lax.psum(body, axis_name=mesh_ax)  67.7 us
    psum x1, waiting for transfers between devices, per_device(): prediction = lax.psum(partial_pred, 'centers')  39.5 us
    psum x1, waiting for transfers between devices, per_device(): lax.psum(lax.psum(body, axis_name=mesh_ax), axis_name=group_axis)  33.7 us
    psum x1, waiting for transfers between devices, per_device(): grads = lax.psum(grads_part, 'batch')  31.3 us
    all_gather x1, blocking collectives, per_device(): lax.all_gather(local_rows, 'centers', axis=0, tiled=True)  31.2 us
    all_gather x1, blocking collectives, per_device(): all_targets = lax.all_gather(local_targets, 'centers', axis=0, tiled=True)  30.8 us
    psum x1, waiting for transfers between devices, per_device(): correction = lax.psum(corr_part, 'batch')  27.9 us
    scatter x1, local copies, waits for them, and re-layouts, per_device(): jnp.zeros((group_size, slots), jnp.int32).at[owner, slot_rank]  19.9 us
  transfers between devices with their start and end apart: 7, of which 6 were waited for; matrix products, arithmetic and copies ran while one was open for 4% of the time, Pallas kernels for 0%

profile of v1, /device:TPU:0, one launch (start us, length us, event | category | flops | bytes accessed | tf_op | source)
XLA Modules:
  0.0 366.0 jit_solution(8851267280370700177)
XLA Ops:
  7.2 0.0 copy-start
  7.2 0.0 copy-start.6
  7.2 0.7 copy-done.6
  7.9 0.1 fusion.4
  8.0 0.2 reduce_window_sum.11
  8.2 0.2 select_reduce_fusion
  8.3 0.0 copy-start.8
  8.4 0.6 broadcast.104
  9.0 0.1 copy-done.8
  9.0 19.9 %scatter_fusion = s32[8,32]{1,0:T(8,128)} fusion(s32[8,32]{1,0:T(8,128)} %broadcast.104, s32[128]{0:T(128)S(1)} %get-tuple-element.8, s32[128]{0:T(128)S(1)} %copy-done.8), kind=kCustom, calls=%fused_computation.4 | custom fusion | bytes 2560 | tf_op jit(solution)/shard_map/scatter | solution.py:83
  28.9 7.4 %all-to-all-start = ((s32[8,1,32]{2,1,0:T(1,128)}), s32[8,1,32]{2,1,0:T(1,128)S(1)}, u32[]{:S(2)}, u32[]{:S(2)}) async-start(s32[8,1,32]{2,1,0:T(1,128)} %bitcast.4), calls=%async_computation | async-start | bytes 8192 | tf_op jit(solution)/shard_map/all_to_all | solution.py:84
  36.3 0.0 all-reduce.6.cloned.1.call-start
  36.4 0.1 multiply_reduce_fusion
  36.6 0.6 gather_fusion
  37.2 31.2 %all-gather = f32[512,128]{1,0:T(8,128)S(1)} all-gather(f32[64,128]{1,0:T(8,128)S(1)} %gather_fusion), channel_id=2, replica_groups=mesh['batch'=4,'centers'=8] {'centers'}, dimensions={0}, use_global_device_ids=true | all-gather | bytes 294912 | tf_op jit(solution)/shard_map/all_gather | solution.py:60
  68.4 0.1 multiply_reduce_fusion.1
  68.6 0.0 copy-start.4
  68.6 8.9 %multiply_add_fusion = f32[512,512]{1,0:T(8,128)S(1)} fusion(f32[512,128]{1,0:T(8,128)S(1)} %all-gather, f32[512,128]{1,0:T(8,128)S(1)} %copy-done.3, f32[512]{0:T(512)S(1)} %multiply_add_fusion.1, f32[512]{0:T(512)S(1)} %multiply_add_fusion.2), kind=kOutput, calls=%fused_computation.11 | convolution fusion | flops 414187520 | bytes 1576960 | tf_op jit(solution)/shard_map/dot_general | solution.py:14
  77.5 0.0 copy-start.2
  77.5 1.8 fusion.8
  79.3 0.0 all-reduce.6.cloned.1.call-update
  79.4 0.0 all-reduce.8.cloned.1.call-start
  79.4 0.2 copy.23
  79.6 0.6 gather_fusion.1
  80.2 30.8 %all-gather.1 = f32[512,64]{1,0:T(8,128)S(1)} all-gather(f32[64,64]{1,0:T(8,128)S(1)} %gather_fusion.1), channel_id=3, replica_groups=mesh['batch'=4,'centers'=8] {'centers'}, dimensions={0}, use_global_device_ids=true | all-gather | bytes 147456 | tf_op jit(solution)/shard_map/all_gather | solution.py:63
  111.1 0.1 copy.24
  111.2 0.0 all-to-all-done
  111.2 0.1 reshape.100
  111.3 39.5 %all-reduce.6.cloned.1.call-done = f32[512,64]{0,1:T(8,128)} async-done(((f32[512,64]{0,1:T(8,128)}), f32[512,64]{0,1:T(8,128)}) %all-reduce.6.cloned.1.call-update) | async-done | bytes 131088 | tf_op jit(solution)/shard_map/psum | solution.py:64
  150.8 0.9 sub.36
  151.7 1.5 convolution_multiply_fusion.1
  153.2 0.0 all-reduce.8.cloned.1.call-update
  153.2 0.0 all-reduce.10.cloned.1.call-start
  153.3 31.3 %all-reduce.8.cloned.1.call-done = f32[512,64]{0,1:T(8,128)} async-done(((f32[512,64]{0,1:T(8,128)}), f32[512,64]{0,1:T(8,128)}) %all-reduce.8.cloned.1.call-update) | async-done | bytes 131088 | tf_op jit(solution)/shard_map/psum | solution.py:76
  184.6 1.0 copy.26
  185.6 0.7 gather_fusion.2
  186.3 0.1 reshape.114
  186.5 12.2 %all_to_all.22 = f32[8,1,2048]{2,1,0:T(1,128)S(1)} all-to-all(f32[8,1,2048]{2,1,0:T(1,128)S(1)} %reshape.114), channel_id=1, replica_groups=mesh['batch'=4,'centers'=8] {'centers'}, dimensions={0} | all-to-all | bytes 131072 | tf_op jit(solution)/shard_map/all_to_all | solution.py:86
  198.7 0.5 broadcast.212
  199.2 0.8 reduce
  200.0 0.1 reshape.115
  200.1 1.2 gather_fusion.3
  201.3 1.1 convolution_bitcast_fusion
  202.5 0.0 all-reduce.10.cloned.1.call-update
  202.5 0.0 all-reduce.12.cloned.1.call-start
  202.5 67.7 %all-reduce.10.cloned.1.call-done = f32[1024,64]{0,1:T(8,128)} async-done(((f32[1024,64]{0,1:T(8,128)}), f32[1024,64]{0,1:T(8,128)}) %all-reduce.10.cloned.1.call-update) | async-done | bytes 262160 | tf_op jit(solution)/shard_map/psum | solution.py:96
  270.2 0.0 all-reduce.12.cloned.1.call-update
  270.3 33.7 %all-reduce.12.cloned.1.call-done = f32[1024,64]{0,1:T(8,128)} async-done(((f32[1024,64]{0,1:T(8,128)}), f32[1024,64]{0,1:T(8,128)}) %all-reduce.12.cloned.1.call-update) | async-done | bytes 262160 | tf_op jit(solution)/shard_map/psum | solution.py:95
  303.9 1.6 convolution_bitcast_fusion.1
  305.6 0.1 copy.27
  305.7 6.9 %scatter_fusion.1 = f32[8,32,64]{2,1,0:T(8,128)S(1)} fusion(f32[8,32,64]{2,1,0:T(8,128)S(1)} %broadcast_in_dim.8, s32[128]{0:T(128)S(1)} %get-tuple-element.8, f32[128,64]{1,0:T(8,128)S(1)} %copy.27), kind=kCustom, calls=%fused_computation.5 | custom fusion | bytes 99328 | tf_op jit(solution)/shard_map/scatter | solution.py:106
  312.6 0.8 reshape.116
  313.3 5.5 %all-to-all-start.2 = ((f32[8,1,2048]{2,1,0:T(1,128)}), f32[8,1,2048]{2,1,0:T(1,128)S(1)}, u32[]{:S(2)}, u32[]{:S(2)}) async-start(f32[8,1,2048]{2,1,0:T(1,128)} %reshape.116), calls=%async_computation.2 | async-start | bytes 131072 | tf_op jit(solution)/shard_map/all_to_all | solution.py:108
  318.8 0.0 all-reduce.14.cloned.1.call-start
  318.9 6.9 %all-to-all-done.2 = f32[8,1,2048]{2,1,0:T(1,128)S(1)} async-done(((f32[8,1,2048]{2,1,0:T(1,128)}), f32[8,1,2048]{2,1,0:T(1,128)S(1)}, u32[]{:S(2)}, u32[]{:S(2)}) %all-to-all-start.2) | async-done | bytes 65568 | tf_op jit(solution)/shard_map/all_to_all | solution.py:108
  325.7 0.8 reduce.1
  326.5 0.1 reshape.117
  326.6 1.7 scatter_custom_fusion.2
  328.4 0.8 copy.28
  329.1 0.0 all-reduce.14.cloned.1.call-update
  329.2 0.1 constant_dynamic-slice_fusion
  329.3 0.7 copy.29
  330.0 27.9 %all-reduce.14.cloned.1.call-done = f32[512,64]{0,1:T(8,128)} async-done(((f32[512,64]{0,1:T(8,128)}), f32[512,64]{0,1:T(8,128)}) %all-reduce.14.cloned.1.call-update) | async-done | bytes 131088 | tf_op jit(solution)/shard_map/psum | solution.py:110
  357.9 1.6 sub.38
  (21 shorter events, 0.1 us)
Async XLA Ops:
  7.2 194.2 %copy-start = (f32[128,1024]{1,0:T(8,128)S(1)}, f32[128,1024]{1,0:T(8,128)}, u32[]{:S(2)}) copy-start(f32[128,1024]{1,0:T(8,128)} %param.14) | copy-start | bytes 1572868
  7.2 0.7 copy-start.6
  8.3 0.7 copy-start.8
  9.0 27.4 %copy-start.3 = (f32[512,128]{1,0:T(8,128)S(1)}, f32[512,128]{1,0:T(8,128)}, u32[]{:S(2)}) copy-start(f32[512,128]{1,0:T(8,128)} %param.12) | copy-start | bytes 786436
  9.0 27.6 %copy-start.5 = (f32[1024,128]{1,0:T(8,128)S(1)}, f32[1024,128]{1,0:T(8,128)}, u32[]{:S(2)}) copy-start(f32[1024,128]{1,0:T(8,128)} %param.9) | copy-start | bytes 1572868
  28.9 7.5 %copy-start.9 = (s32[64]{0:T(128)S(1)}, s32[64]{0:T(128)}, u32[]{:S(2)}) copy-start(s32[64]{0:T(128)} %param.11) | copy-start | bytes 772
  28.9 82.3 %all-to-all-start = ((s32[8,1,32]{2,1,0:T(1,128)}), s32[8,1,32]{2,1,0:T(1,128)S(1)}, u32[]{:S(2)}, u32[]{:S(2)}) async-start(s32[8,1,32]{2,1,0:T(1,128)} %bitcast.4), calls=%async_computation | async-start | bytes 8192 | tf_op jit(solution)/shard_map/all_to_all | solution.py:84
  36.3 114.5 %all-reduce.6.cloned.1.call-start = ((), (), s32[]{:S(2)}) async-start(), calls=%async_computation.3 | async-start | bytes 262144 | tf_op jit(solution)/shard_map/psum | solution.py:64
  68.6 8.9 %copy-start.4 = (f32[512,64]{0,1:T(8,128)S(1)}, f32[512,64]{0,1:T(8,128)}, u32[]{:S(2)}) copy-start(f32[512,64]{0,1:T(8,128)} %param.13) | copy-start | bytes 393220
  77.5 1.9 copy-start.2
  79.4 105.2 %all-reduce.8.cloned.1.call-start = ((), (), s32[]{:S(2)}) async-start(), calls=%async_computation.4 | async-start | bytes 262144 | tf_op jit(solution)/shard_map/psum | solution.py:76
  153.2 117.0 %all-reduce.10.cloned.1.call-start = ((), (), s32[]{:S(2)}) async-start(), calls=%async_computation.5 | async-start | bytes 524288 | tf_op jit(solution)/shard_map/psum | solution.py:96
  202.5 101.4 %all-reduce.12.cloned.1.call-start = ((), (), s32[]{:S(2)}) async-start(), calls=%async_computation.6 | async-start | bytes 524288 | tf_op jit(solution)/shard_map/psum | solution.py:95
  270.2 33.7 %copy-start.7 = (f32[1024]{0:T(1024)S(1)}, f32[1024]{0:T(1024)}, u32[]{:S(2)}) copy-start(f32[1024]{0:T(1024)} %param.15) | copy-start | bytes 12292
  313.3 12.4 %all-to-all-start.2 = ((f32[8,1,2048]{2,1,0:T(1,128)}), f32[8,1,2048]{2,1,0:T(1,128)S(1)}, u32[]{:S(2)}, u32[]{:S(2)}) async-start(f32[8,1,2048]{2,1,0:T(1,128)} %reshape.116), calls=%async_computation.2 | async-start | bytes 131072 | tf_op jit(solution)/shard_map/all_to_all | solution.py:108
  318.8 39.0 %all-reduce.14.cloned.1.call-start = ((), (), s32[]{:S(2)}) async-start(), calls=%async_computation.7 | async-start | bytes 262144 | tf_op jit(solution)/shard_map/psum | solution.py:110
  329.1 28.7 %copy-start.1 = (f32[512,64]{0,1:T(8,128)S(1)}, f32[512,64]{0,1:T(8,128)}, u32[]{:S(2)}) copy-start(f32[512,64]{0,1:T(8,128)} %all-reduce.8.cloned.1.call-done) | copy-start | bytes 393220
Sparse Core Ops, SparseCore 0:
  79.5 71.2 all-reduce.5
  153.7 30.8 all-reduce.7
  202.6 67.5 all-reduce.9
  272.4 31.4 all-reduce.11
  329.3 28.5 all-reduce.13
